TPU v7x, 256 devices: a whole 4x4x8 slice. The times are simulated.
256 devices in a mesh: row: 16 (over y_hi, x, core), col: 16 (over z, y_lo).
Axes of the slice: x: 4, y: 4 (y_hi: 2, y_lo: 2; y = y_hi * 2 + y_lo), z: 8, core: 2. Of those that a mesh axis runs over, the one named last changes fastest.
Arguments:
- hessenberg: float32 [16384, 16384], P('row', 'col'), may hold values from -6 to 6, as said below
- factors: float32 [3, 32, 512, 512], P(None, 'row', 'col'), may hold values from -1 to 1, as said below
- active: int32 [3, 32], replicated, may hold values 0 or 1
Outputs:
- updated_slab: float32 [16384, 16384], P('row', 'col')
Inputs may be any that keep to these rules, and one draw needn't show every extreme that they name: `hessenberg`: in global order, zero below the first subdiagonal. Each factors[f, s] is orthogonal up to float32 rounding.
All inputs are finite; a program needn't handle non-finite values.
Results may differ from a plain program's by a relative error of at most 0.0001.
Values sent between devices are 32-bit elements; how exact they have to be, the bound alone decides.
A program may use at most 64 MiB of HBM per device.

v0:
```python
import jax
import jax.numpy as jnp
from jax import lax
from jax.sharding import PartitionSpec as P

PRECISE = lax.Precision.HIGHEST


def passed_along(value, axis, steps):
    count = lax.axis_size(axis)
    pairs = [(source, (source + steps) % count) for source in range(count)]
    return lax.ppermute(value, axis, pairs)


def left_apply(factor, stacked):
    return jnp.einsum("kab,kan->kbn", factor, stacked, precision=PRECISE)


def right_apply(stacked, factor):
    return jnp.einsum("nka,kab->nkb", stacked, factor, precision=PRECISE)


def effective(factor, flag_row):
    identity = jnp.eye(factor.shape[-1], dtype=jnp.float32)
    return jnp.where(flag_row[:, None, None] > 0, factor, identity)


def wrap_fix(received, at_edge, offset_by, along_dim):
    return jnp.where(at_edge, jnp.roll(received, offset_by, axis=along_dim), received)


def sort_columns(collected, grid_rows):
    phases, all_blocks, pieces, window = collected.shape
    natural = collected.reshape(
        phases, grid_rows, all_blocks // grid_rows, pieces, window
    ).transpose(0, 2, 1, 3, 4)
    return natural.transpose(0, 2, 1, 3, 4)


def local(hessenberg, factors, active):
    rows_here, cols_here = hessenberg.shape
    window = factors.shape[-1]
    half_win = window // 2
    phases = factors.shape[0]
    grid_rows = lax.axis_size("row")
    grid_cols = lax.axis_size("col")
    row_index = lax.axis_index("row")
    col_index = lax.axis_index("col")
    row_blocks = rows_here // window
    col_blocks = cols_here // window
    all_blocks = row_blocks * grid_rows
    slot_row = jnp.arange(row_blocks, dtype=jnp.int32) * grid_rows + row_index
    slot_col = jnp.arange(col_blocks, dtype=jnp.int32) * grid_cols + col_index
    within = jnp.arange(window, dtype=jnp.int32)
    glob_row = (slot_row[:, None] * window + within[None, :]).reshape(rows_here)
    glob_col = (slot_col[:, None] * window + within[None, :]).reshape(cols_here)
    current = hessenberg
    for phase_idx in range(phases):
        chosen = factors[phase_idx : phase_idx + 1]
        row_raw = lax.all_gather(chosen, "col", axis=2, tiled=True)[0]
        gathered = lax.all_gather(chosen, "row", axis=1, tiled=True)
        col_raw = lax.all_to_all(
            sort_columns(gathered, grid_rows), "col", split_axis=1, concat_axis=3, tiled=True
        )
        col_raw = col_raw.reshape(col_blocks, window, window)
        flag_all = active[phase_idx]
        row_flag = jnp.take(flag_all, slot_row)
        col_flag = jnp.take(flag_all, slot_col)
        if phase_idx % 2 == 1:
            row_flag = jnp.where(slot_row < all_blocks - 1, row_flag, 0)
            col_flag = jnp.where(slot_col < all_blocks - 1, col_flag, 0)
        row_factor = effective(row_raw, row_flag)
        col_factor = effective(col_raw, col_flag)
        blocks = current.reshape(row_blocks, window, cols_here)
        if phase_idx % 2 == 0:
            updated = left_apply(row_factor, blocks)
            keep_mask = glob_col[None, :] >= (slot_row[:, None] + 1) * window
            current = jnp.where(keep_mask[:, None, :], updated, blocks).reshape(
                rows_here, cols_here
            )
            columns = current.reshape(rows_here, col_blocks, window)
            updated = right_apply(columns, col_factor)
            keep_mask = glob_row[:, None] < slot_col[None, :] * window
            current = jnp.where(keep_mask[:, :, None], updated, columns).reshape(
                rows_here, cols_here
            )
        else:
            top_half = blocks[:, :half_win]
            bottoms = blocks[:, half_win:]
            from_below = wrap_fix(
                passed_along(top_half, "row", -1), row_index == grid_rows - 1, -1, 0
            )
            stacked = jnp.concatenate([bottoms, from_below], axis=1)
            updated = left_apply(row_factor, stacked)
            keep_mask = glob_col[None, :] >= slot_row[:, None] * window + window + half_win
            updated = jnp.where(keep_mask[:, None, :], updated, stacked)
            returned = wrap_fix(passed_along(updated[:, half_win:], "row", 1), row_index == 0, 1, 0)
            current = jnp.concatenate([returned, updated[:, :half_win]], axis=1).reshape(
                rows_here, cols_here
            )
            columns = current.reshape(rows_here, col_blocks, window)
            left_half = columns[:, :, :half_win]
            right_half = columns[:, :, half_win:]
            from_right = wrap_fix(
                passed_along(left_half, "col", -1), col_index == grid_cols - 1, -1, 1
            )
            stacked = jnp.concatenate([right_half, from_right], axis=2)
            updated = right_apply(stacked, col_factor)
            keep_mask = glob_row[:, None] < slot_col[None, :] * window + half_win
            updated = jnp.where(keep_mask[:, :, None], updated, stacked)
            returned = wrap_fix(
                passed_along(updated[:, :, half_win:], "col", 1), col_index == 0, 1, 1
            )
            current = jnp.concatenate([returned, updated[:, :, :half_win]], axis=2).reshape(
                rows_here, cols_here
            )
    return current


def solution(mesh):
    return jax.shard_map(
        local,
        mesh=mesh,
        in_specs=(P("row", "col"), P(None, "row", "col", None), P()),
        out_specs=P("row", "col"),
        check_vma=False,
    )
```

profile of v0, /device:TPU:6, one launch (start us, length us, event | category | flops | bytes accessed | tf_op | source)
XLA Modules:
  0.0 637.7 jit_solution(7800001573734973021)
XLA Ops:
  6.5 1.9 slice_bitcast_fusion
  8.5 0.7 all-gather.17.cloned.1.call-update
  9.2 57.1 %all-gather.15.cloned.1.call-done = f32[1,32,32,512]{3,2,0,1:T(8,128)} async-done(((f32[1,2,32,512]{3,2,0,1:T(8,128)}), f32[1,32,32,512]{3,2,0,1:T(8,128)}) %all-gather.15.cloned.1.call-update) | async-done | bytes 2097168 | tf_op jit(solution)/shard_map/all_gather | solution.py:61
  66.3 7.3 %all-to-all-start.2 = ((f32[1,16,2,32,512]{4,3,2,0,1:T(8,128)}), f32[1,16,2,32,512]{4,3,2,0,1:T(8,128)S(1)}, u32[]{:S(2)}, u32[]{:S(2)}) async-start(f32[1,16,2,32,512]{4,3,2,0,1:T(8,128)} %bitcast.71), calls=%async_computation.2 | async-start | bytes 4194304 | tf_op jit(solution)/shard_map/all_to_all | solution.py:62
  73.6 0.7 all-gather.13.cloned.1.call-update
  74.6 0.6 gather_fusion.5
  75.2 0.6 gather_fusion.4
  76.2 91.1 %all-gather.17.cloned.1.call-done = f32[1,2,512,512]{3,2,1,0:T(8,128)} async-done(((f32[1,2,32,512]{3,2,1,0:T(8,128)}), f32[1,2,512,512]{3,2,1,0:T(8,128)}) %all-gather.17.cloned.1.call-update) | async-done | bytes 2097168 | tf_op jit(solution)/shard_map/all_gather | solution.py:60
  167.3 11.6 %convolution_select_fusion.1 = f32[2,512,1024]{2,1,0:T(8,128)} fusion(f32[2,512,1024]{2,1,0:T(8,128)} %bitcast.69, f32[1,2,512,512]{3,2,1,0:T(8,128)} %all-gather.17.cloned.1.call-done, pred[2,1024]{1,0:T(4,128)(4,1)S(1)} %get-tuple-element.30, f32[512,512]{1,0:T(8,128)S(1)} %fusion.20, pred[2]{0:T(512)(128)(4,1)S(1)} %select_compare_fusion), kind=kOutput, calls=%fused_computation.17 | convolution fusion | flops 6444023808 | bytes 11536386 | tf_op jit(solution)/shard_map/kab,kan->kbn/dot_general | solution.py:16
  178.9 6.6 %reshape_reshape.15 = f32[1024,2,512]{2,1,0:T(2,128)} reshape(f32[2,512,1024]{2,1,0:T(8,128)} %convolution_select_fusion.1) | data formatting | bytes 8388608 | tf_op jit(solution)/shard_map/reshape;reshape | solution.py:81
  185.5 7.2 %copy.56 = f32[1024,2,512]{0,2,1:T(8,128)} copy(f32[1024,2,512]{2,1,0:T(2,128)} %reshape_reshape.15) | data formatting | bytes 8388608 | tf_op jit(solution)/shard_map/reshape;reshape | solution.py:81
  192.7 0.2 copy.52
  192.9 2.0 copy-done
  194.9 8.8 %bitcast_select_fusion.2 = f32[1024,2,512]{0,2,1:T(8,128)} fusion(f32[1024,2,512]{0,2,1:T(8,128)S(1)} %copy-done, f32[2,512,512]{2,1,0:T(8,128)S(1)} %bitcast.67, pred[1024,2]{0,1:T(4,128)(4,1)S(1)} %get-tuple-element.28, f32[512,512]{1,0:T(8,128)S(1)} %fusion.20, pred[2]{0:T(512)(128)(4,1)S(1)} %select_compare_fusion.1), kind=kOutput, calls=%fused_computation.12 | convolution fusion | flops 6444023808 | bytes 11536386 | tf_op jit(solution)/shard_map/nka,kab->nkb/dot_general | solution.py:20
  203.7 6.6 %reshape_reshape.16 = f32[2,512,1024]{1,0,2:T(2,128)} reshape(f32[1024,2,512]{0,2,1:T(8,128)} %bitcast_select_fusion.2) | data formatting | bytes 8388608 | tf_op jit(solution)/shard_map/reshape;reshape | solution.py:74
  210.3 5.0 fusion.30
  215.3 2.9 copy.79
  218.2 0.2 collective-permute-start
  218.4 0.6 gather_fusion.3
  219.1 4.1 copy.78
  223.2 19.0 %collective-permute-done = f32[2,256,1024]{2,1,0:T(8,128)S(1)} collective-permute-done((f32[2,256,1024]{2,1,0:T(8,128)}, f32[2,256,1024]{2,1,0:T(8,128)S(1)}, u32[]{:S(2)}, u32[]{:S(2)}) %collective-permute-start) | collective-permute-done | bytes 2097184 | tf_op jit(solution)/shard_map/ppermute | solution.py:12
  242.3 1.2 copy-done.1
  243.5 1.8 maximum_select_fusion
  245.4 18.9 %all-gather.13.cloned.1.call-done = f32[1,2,512,512]{3,2,1,0:T(8,128)} async-done(((f32[1,2,32,512]{3,2,1,0:T(8,128)}), f32[1,2,512,512]{3,2,1,0:T(8,128)}) %all-gather.13.cloned.1.call-update) | async-done | bytes 2097168 | tf_op jit(solution)/shard_map/all_gather | solution.py:60
  264.3 10.6 %fusion.1 = f32[2,512,1024]{2,1,0:T(8,128)S(1)} fusion(f32[2,256,1024]{2,1,0:T(8,128)S(1)} %maximum_select_fusion, f32[2,256,1024]{2,1,0:T(8,128)} %copy.78, pred[2,1024]{1,0:T(4,128)(4,1)S(1)} %get-tuple-element.29, f32[1,2,512,512]{3,2,1,0:T(8,128)} %all-gather.13.cloned.1.call-done, f32[512,512]{1,0:T(8,128)S(1)} %fusion.20, pred[2]{0:T(512)(128)(4,1)S(1)} %fusion.22), kind=kOutput, calls=%fused_computation.14 | convolution fusion | flops 6446120960 | bytes 11536386 | tf_op jit(solution)/shard_map/kab,kan->kbn/dot_general | solution.py:16
  274.9 2.3 fusion.29
  277.3 44.1 %all-gather.11.cloned.1.call-done = f32[1,32,32,512]{3,2,0,1:T(8,128)} async-done(((f32[1,2,32,512]{3,2,0,1:T(8,128)}), f32[1,32,32,512]{3,2,0,1:T(8,128)}) %all-gather.11.cloned.1.call-update) | async-done | bytes 2097168 | tf_op jit(solution)/shard_map/all_gather | solution.py:61
  321.4 7.6 %all-to-all-start.1 = ((f32[1,16,2,32,512]{4,3,2,0,1:T(8,128)}), f32[1,16,2,32,512]{4,3,2,0,1:T(8,128)}, u32[]{:S(2)}, u32[]{:S(2)}) async-start(f32[1,16,2,32,512]{4,3,2,0,1:T(8,128)} %bitcast.72), calls=%async_computation.1 | async-start | bytes 4194304 | tf_op jit(solution)/shard_map/all_to_all | solution.py:62
  329.0 0.1 fusion.33
  329.2 0.4 maximum_select_fusion.1
  329.6 1.2 copy-done.4
  330.8 2.5 pad_maximum_fusion.1
  333.3 6.6 %reshape_reshape.17 = f32[1024,2,512]{2,1,0:T(2,128)} reshape(f32[2,512,1024]{2,1,0:T(8,128)} %pad_maximum_fusion.1) | data formatting | bytes 8388608 | tf_op jit(solution)/shard_map/reshape;reshape | solution.py:101
  339.9 5.0 fusion.28
  344.9 1.5 copy.81
  346.4 4.1 collective-permute-start.2
  350.5 85.0 %all-gather.7.cloned.1.call-done = f32[1,32,32,512]{3,2,0,1:T(8,128)} async-done(((f32[1,2,32,512]{3,2,0,1:T(8,128)}), f32[1,32,32,512]{3,2,0,1:T(8,128)}) %all-gather.7.cloned.1.call-update) | async-done | bytes 2097168 | tf_op jit(solution)/shard_map/all_gather | solution.py:61
  435.5 6.6 %all-to-all-start = ((f32[1,16,2,32,512]{4,3,2,0,1:T(8,128)}), f32[1,16,2,32,512]{4,3,2,0,1:T(8,128)}, u32[]{:S(2)}, u32[]{:S(2)}) async-start(f32[1,16,2,32,512]{4,3,2,0,1:T(8,128)} %bitcast.70), calls=%async_computation | async-start | bytes 4194304 | tf_op jit(solution)/shard_map/all_to_all | solution.py:62
  442.1 0.5 all-gather.9.cloned.1.call-update
  442.7 0.6 gather_fusion.2
  443.3 2.0 copy.49
  445.4 0.2 copy-done.3
  445.6 0.2 copy.80
  445.7 0.1 fusion.32
  445.9 0.3 maximum_select_fusion.2
  446.2 7.8 %bitcast_select_fusion.1 = f32[1024,2,512]{2,0,1:T(8,128)S(1)} fusion(f32[1024,2,256]{2,0,1:T(8,128)S(1)} %maximum_select_fusion.2, f32[1024,2,256]{2,0,1:T(8,128)S(1)} %copy.80, pred[1024,2]{0,1:T(4,128)(4,1)S(1)} %get-tuple-element.27, f32[2,512,512]{2,1,0:T(8,128)S(1)} %bitcast.68, f32[512,512]{1,0:T(8,128)S(1)} %fusion.20, pred[2]{0:T(512)(128)(4,1)S(1)} %fusion.21), kind=kOutput, calls=%fused_computation.11 | convolution fusion | flops 6446120960 | bytes 11536386 | tf_op jit(solution)/shard_map/nka,kab->nkb/dot_general | solution.py:20
  453.9 2.4 fusion.27
  456.3 2.0 collective-permute-start.3
  458.4 0.6 gather_fusion.1
  459.0 0.6 gather_fusion
  459.7 36.5 %all-to-all-done = f32[1,16,2,32,512]{4,3,2,0,1:T(8,128)} async-done(((f32[1,16,2,32,512]{4,3,2,0,1:T(8,128)}), f32[1,16,2,32,512]{4,3,2,0,1:T(8,128)}, u32[]{:S(2)}, u32[]{:S(2)}) %all-to-all-start) | async-done | bytes 2097184 | tf_op jit(solution)/shard_map/all_to_all | solution.py:62
  496.1 3.3 copy.46
  499.4 49.3 %collective-permute-done.3 = f32[1024,2,256]{2,0,1:T(8,128)S(1)} collective-permute-done((f32[1024,2,256]{2,0,1:T(8,128)}, f32[1024,2,256]{2,0,1:T(8,128)S(1)}, u32[]{:S(2)}, u32[]{:S(2)}) %collective-permute-start.3) | collective-permute-done | bytes 2097184 | tf_op jit(solution)/shard_map/ppermute | solution.py:12
  548.9 0.4 maximum_select_fusion.3
  549.3 1.2 copy-done.5
  550.5 0.6 pad_maximum_fusion.3
  551.1 5.3 copy.64
  556.4 6.6 %reshape_reshape.18 = f32[2,512,1024]{2,1,0:T(8,128)} reshape(f32[1024,2,512]{2,1,0:T(2,128)} %copy.64) | data formatting | bytes 8388608 | tf_op jit(solution)/shard_map/reshape;reshape | solution.py:74
  563.0 25.0 %all-gather.9.cloned.1.call-done = f32[1,2,512,512]{3,2,0,1:T(8,128)} async-done(((f32[1,2,32,512]{3,2,0,1:T(8,128)}), f32[1,2,512,512]{3,2,0,1:T(8,128)}) %all-gather.9.cloned.1.call-update) | async-done | bytes 2097168 | tf_op jit(solution)/shard_map/all_gather | solution.py:60
  587.9 11.6 %convolution_select_fusion = f32[2,512,1024]{2,1,0:T(8,128)} fusion(f32[2,512,1024]{2,1,0:T(8,128)} %reshape_reshape.18, f32[1,2,512,512]{3,2,0,1:T(8,128)} %all-gather.9.cloned.1.call-done, pred[2,1024]{1,0:T(4,128)(4,1)S(1)} %get-tuple-element.30, f32[512,512]{1,0:T(8,128)S(1)} %fusion.20, pred[2]{0:T(512)(128)(4,1)S(1)} %select_compare_fusion.2), kind=kOutput, calls=%fused_computation.16 | convolution fusion | flops 6444023808 | bytes 11536386 | tf_op jit(solution)/shard_map/kab,kan->kbn/dot_general | solution.py:16
  599.5 6.6 %reshape_reshape.19 = f32[1024,2,512]{2,1,0:T(2,128)} reshape(f32[2,512,1024]{2,1,0:T(8,128)} %convolution_select_fusion) | data formatting | bytes 8388608 | tf_op jit(solution)/shard_map/reshape;reshape | solution.py:81
  606.1 7.3 %copy.68 = f32[1024,2,512]{0,2,1:T(8,128)} copy(f32[1024,2,512]{2,1,0:T(2,128)} %reshape_reshape.19) | data formatting | bytes 8388608 | tf_op jit(solution)/shard_map/reshape;reshape | solution.py:81
  613.4 11.9 %bitcast_select_fusion = f32[1024,2,512]{0,2,1:T(8,128)} fusion(f32[1024,2,512]{0,2,1:T(8,128)} %copy.68, f32[2,512,512]{2,1,0:T(8,128)S(1)} %bitcast.66, pred[1024,2]{0,1:T(4,128)(4,1)S(1)} %get-tuple-element.28, f32[512,512]{1,0:T(8,128)S(1)} %fusion.20, pred[2]{0:T(512)(128)(4,1)S(1)} %select_compare_fusion.3), kind=kOutput, calls=%fused_computation.10 | convolution fusion | flops 6444023808 | bytes 11536386 | tf_op jit(solution)/shard_map/nka,kab->nkb/dot_general | solution.py:20
  625.3 5.3 copy.69
  (45 shorter events, 1.1 us)
Async XLA Ops:
  6.5 59.7 %all-gather.15.cloned.1.call-start = ((), (), s32[]{:S(2)}) async-start(), calls=%async_computation.7 | async-start | bytes 2228224 | tf_op jit(solution)/shard_map/all_gather | solution.py:61
  8.4 158.9 %all-gather.17.cloned.1.call-start = ((), (), s32[]{:S(2)}) async-start(), calls=%async_computation.8 | async-start | bytes 2228224 | tf_op jit(solution)/shard_map/all_gather | solution.py:60
  66.3 8.3 %copy-start.6 = (s32[3,32]{1,0:T(4,128)S(1)}, s32[3,32]{1,0:T(4,128)}, u32[]{:S(2)}) copy-start(s32[3,32]{1,0:T(4,128)} %param.7) | copy-start | bytes 1156
  66.3 126.4 %all-to-all-start.2 = ((f32[1,16,2,32,512]{4,3,2,0,1:T(8,128)}), f32[1,16,2,32,512]{4,3,2,0,1:T(8,128)S(1)}, u32[]{:S(2)}, u32[]{:S(2)}) async-start(f32[1,16,2,32,512]{4,3,2,0,1:T(8,128)} %bitcast.71), calls=%async_computation.2 | async-start | bytes 4194304 | tf_op jit(solution)/shard_map/all_to_all | solution.py:62
  73.6 190.7 %all-gather.13.cloned.1.call-start = ((), (), s32[]{:S(2)}) async-start(), calls=%async_computation.6 | async-start | bytes 2228224 | tf_op jit(solution)/shard_map/all_gather | solution.py:60
  74.3 247.1 %all-gather.11.cloned.1.call-start = ((), (), s32[]{:S(2)}) async-start(), calls=%async_computation.5 | async-start | bytes 2228224 | tf_op jit(solution)/shard_map/all_gather | solution.py:61
  192.7 2.2 copy-start
  218.2 24.0 %collective-permute-start = (f32[2,256,1024]{2,1,0:T(8,128)}, f32[2,256,1024]{2,1,0:T(8,128)S(1)}, u32[]{:S(2)}, u32[]{:S(2)}) collective-permute-start(f32[2,256,1024]{2,1,0:T(8,128)} %copy.79), channel_id=1, source_target_pairs={{0,240},{16,0},{32,16},{48,32},{64,48},{80,64},{96,80},{112,96},{1... | collective-permute-start | bytes 6291464 | tf_op jit(solution)/shard_map/ppermute | solution.py:12
  218.4 217.1 %all-gather.7.cloned.1.call-start = ((), (), s32[]{:S(2)}) async-start(), calls=%async_computation.3 | async-start | bytes 2228224 | tf_op jit(solution)/shard_map/all_gather | solution.py:61
  242.2 1.3 copy-start.1
  277.2 51.8 %collective-permute-start.1 = (f32[2,256,1024]{2,1,0:T(8,128)}, f32[2,256,1024]{2,1,0:T(8,128)S(1)}, u32[]{:S(2)}, u32[]{:S(2)}) collective-permute-start(f32[2,256,1024]{2,1,0:T(8,128)} %get-tuple-element.10), channel_id=1, source_target_pairs={{0,16},{16,32},{32,48},{48,64},{64,80},{80,96},{96,112},{112,128},... | collective-permute-start | bytes 6291464 | tf_op jit(solution)/shard_map/ppermute | solution.py:12
  321.4 114.1 %all-to-all-start.1 = ((f32[1,16,2,32,512]{4,3,2,0,1:T(8,128)}), f32[1,16,2,32,512]{4,3,2,0,1:T(8,128)}, u32[]{:S(2)}, u32[]{:S(2)}) async-start(f32[1,16,2,32,512]{4,3,2,0,1:T(8,128)} %bitcast.72), calls=%async_computation.1 | async-start | bytes 4194304 | tf_op jit(solution)/shard_map/all_to_all | solution.py:62
  329.2 1.6 copy-start.4
  346.4 99.4 %collective-permute-start.2 = (f32[1024,2,256]{2,0,1:T(8,128)}, f32[1024,2,256]{2,0,1:T(8,128)S(1)}, u32[]{:S(2)}, u32[]{:S(2)}) collective-permute-start(f32[1024,2,256]{2,0,1:T(8,128)} %copy.81), channel_id=1, source_target_pairs={{0,15},{1,0},{2,1},{3,2},{4,3},{5,4},{6,5},{7,6},{8,7},{9,8},{10,9... | collective-permute-start | bytes 6291464 | tf_op jit(solution)/shard_map/ppermute | solution.py:12
  435.5 60.6 %all-to-all-start = ((f32[1,16,2,32,512]{4,3,2,0,1:T(8,128)}), f32[1,16,2,32,512]{4,3,2,0,1:T(8,128)}, u32[]{:S(2)}, u32[]{:S(2)}) async-start(f32[1,16,2,32,512]{4,3,2,0,1:T(8,128)} %bitcast.70), calls=%async_computation | async-start | bytes 4194304 | tf_op jit(solution)/shard_map/all_to_all | solution.py:62
  442.1 145.8 %all-gather.9.cloned.1.call-start = ((), (), s32[]{:S(2)}) async-start(), calls=%async_computation.4 | async-start | bytes 2228224 | tf_op jit(solution)/shard_map/all_gather | solution.py:60
  443.3 2.2 copy-start.3
  456.3 92.4 %collective-permute-start.3 = (f32[1024,2,256]{2,0,1:T(8,128)}, f32[1024,2,256]{2,0,1:T(8,128)S(1)}, u32[]{:S(2)}, u32[]{:S(2)}) collective-permute-start(f32[1024,2,256]{2,0,1:T(8,128)} %get-tuple-element.6), channel_id=1, source_target_pairs={{0,1},{1,2},{2,3},{3,4},{4,5},{5,6},{6,7},{7,8},{8,9},{9,10},{10,1... | collective-permute-start | bytes 6291464 | tf_op jit(solution)/shard_map/ppermute | solution.py:12
  548.9 1.6 copy-start.5
  606.1 7.3 %copy-start.2 = (f32[1,1,2,16,32,512]{5,4,3,2,1,0:T(8,128)S(1)}, f32[1,1,2,16,32,512]{5,4,3,2,1,0:T(8,128)}, u32[]{:S(2)}) copy-start(f32[1,1,2,16,32,512]{5,4,3,2,1,0:T(8,128)} %copy.46) | copy-start | bytes 6291460
Sparse Core Ops, SparseCore 0:
  10.1 56.1 all-gather.14
  68.1 99.2 all-gather.16
  169.1 95.1 all-gather.12
  266.9 54.4 all-gather.10
  324.0 111.4 all-gather.6
  444.4 143.4 all-gather.8
where the time goes:
time: 648 us; the launch traced here: 638 us
  waiting for transfers between devices  428 us (66%)
  local copies, waits for them, and re-layouts  98.9 us (15%)
  matrix products  62.3 us (10%)
  starting transfers between devices  28 us (4%)
  between operations  13.9 us (2%)
  other arithmetic  6.62 us (1%)
    all_gather x3, waiting for transfers between devices, local(): gathered = lax.all_gather(chosen, 'row', axis=1, tiled=True)  186 us
    all_gather x3, waiting for transfers between devices, local(): row_raw = lax.all_gather(chosen, 'col', axis=2, tiled=True)[0]  135 us
    ppermute x4, waiting for transfers between devices, passed_along(): return lax.ppermute(value, axis, pairs)  68.3 us
    all_to_all x3, waiting for transfers between devices, local(): lax.all_to_all(sort_columns(gathered, grid_rows), 'col', split_axis=1, co...  36.5 us
    another operation x5, local copies, waits for them, and re-layouts, local(): columns = current.reshape(rows_here, col_blocks, window)  34.2 us
    dot_general x3, matrix products, left_apply(): return jnp.einsum('kab,kan->kbn', factor, stacked, precision=PRECISE)  33.8 us
    dot_general x3, matrix products, right_apply(): return jnp.einsum('nka,kab->nkb', stacked, factor, precision=PRECISE)  28.4 us
    all_to_all x3, starting transfers between devices, local(): lax.all_to_all(sort_columns(gathered, grid_rows), 'col', split_axis=1, co...  21.5 us
  transfers between devices with their start and end apart: 13, of which 9 were waited for; matrix products, arithmetic and copies ran while one was open for 18% of the time, Pallas kernels for 0%

commit v1 on v0

--- a/solution.py
+++ b/solution.py
@@ -59,8 +59,16 @@
         chosen = factors[phase_idx : phase_idx + 1]
         row_raw = lax.all_gather(chosen, "col", axis=2, tiled=True)[0]
         gathered = lax.all_gather(chosen, "row", axis=1, tiled=True)
-        col_raw = lax.all_to_all(
-            sort_columns(gathered, grid_rows), "col", split_axis=1, concat_axis=3, tiled=True
+        col_raw = jnp.concatenate(
+            lax.all_to_all(
+                jnp.stack(
+                    jnp.split(sort_columns(gathered, grid_rows), lax.axis_size("col"), axis=1)
+                ),
+                "col",
+                0,
+                0,
+            ),
+            axis=3,
         )
         col_raw = col_raw.reshape(col_blocks, window, window)
         flag_all = active[phase_idx]

time: 648 us -> 681 us (1.051)
  the two profiles are of different devices: /device:TPU:6 before, /device:TPU:170 now
where the time goes in v1:
time: 681 us; the launch traced here: 670 us
  waiting for transfers between devices  384 us (56%)
  local copies, waits for them, and re-layouts  160 us (23%)
  matrix products  62.1 us (9%)
  starting transfers between devices  43.2 us (6%)
  between operations  14.1 us (2%)
    all_gather x3, waiting for transfers between devices, local(): gathered = lax.all_gather(chosen, 'row', axis=1, tiled=True)  160 us
    ppermute x4, waiting for transfers between devices, passed_along(): return lax.ppermute(value, axis, pairs)  116 us
    all_gather x3, waiting for transfers between devices, local(): row_raw = lax.all_gather(chosen, 'col', axis=2, tiled=True)[0]  86.8 us
    unnamed x70, local copies, waits for them, and re-layouts  74.3 us
    all_to_all x3, starting transfers between devices, local(): lax.all_to_all(jnp.stack(jnp.split(sort_columns(gathered, grid_rows), lax...  35.3 us
    another operation x5, local copies, waits for them, and re-layouts, local(): columns = current.reshape(rows_here, col_blocks, window)  34.3 us
    dot_general x3, matrix products, left_apply(): return jnp.einsum('kab,kan->kbn', factor, stacked, precision=PRECISE)  34 us
    dot_general x3, matrix products, right_apply(): return jnp.einsum('nka,kab->nkb', stacked, factor, precision=PRECISE)  28.1 us
  transfers between devices with their start and end apart: 13, of which 9 were waited for; matrix products, arithmetic and copies ran while one was open for 27% of the time, Pallas kernels for 0%

profile of v1, /device:TPU:170, one launch (start us, length us, event | category | flops | bytes accessed | tf_op | source)
XLA Modules:
  0.0 670.3 jit_solution(674121592610823925)
XLA Ops:
  6.5 1.9 slice_bitcast_fusion.48
  11.1 52.4 %all-gather.15.cloned.1.call-done = f32[1,32,32,512]{3,2,0,1:T(8,128)} async-done(((f32[1,2,32,512]{3,2,0,1:T(8,128)}), f32[1,32,32,512]{3,2,0,1:T(8,128)}) %all-gather.15.cloned.1.call-update) | async-done | bytes 2097168 | tf_op jit(solution)/shard_map/all_gather | solution.py:61
  63.5 1.7 fusion.36
  65.2 1.6 fusion.35
  69.9 1.6 fusion.32
  71.5 1.6 fusion.31
  73.0 1.6 fusion.30
  74.6 1.6 fusion.29
  81.4 8.2 %all-to-all-start.2 = ((f32[16,1,1,2,32,512]{5,4,3,2,1,0:T(8,128)}), f32[16,1,1,2,32,512]{5,4,3,2,1,0:T(8,128)S(1)}, u32[]{:S(2)}, u32[]{:S(2)}) async-start(f32[16,1,1,2,32,512]{5,4,3,2,1,0:T(8,128)} %fusion.21), calls=%async_computation.2 | async-start | bytes 4194304 | tf_op jit(solution)/shard_map/all_to_all | solution.py:63
  92.1 74.6 %all-gather.17.cloned.1.call-done = f32[1,2,512,512]{3,2,1,0:T(8,128)} async-done(((f32[1,2,32,512]{3,2,1,0:T(8,128)}), f32[1,2,512,512]{3,2,1,0:T(8,128)}) %all-gather.17.cloned.1.call-update) | async-done | bytes 2097168 | tf_op jit(solution)/shard_map/all_gather | solution.py:60
  166.7 11.8 %convolution_select_fusion.1 = f32[2,512,1024]{2,1,0:T(8,128)} fusion(f32[2,512,1024]{2,1,0:T(8,128)} %bitcast.249, f32[1,2,512,512]{3,2,1,0:T(8,128)} %all-gather.17.cloned.1.call-done, pred[2,1024]{1,0:T(4,128)(4,1)S(1)} %get-tuple-element.30, f32[512,512]{1,0:T(8,128)S(1)} %fusion.20, pred[2]{0:T(512)(128)(4,1)S(1)} %select_compare_fusion), kind=kOutput, calls=%fused_computation.17 | convolution fusion | flops 6444023808 | bytes 11536386 | tf_op jit(solution)/shard_map/kab,kan->kbn/dot_general | solution.py:16
  178.5 6.6 reshape_reshape.27
  185.1 7.2 %copy.132 = f32[1024,2,512]{0,2,1:T(8,128)} copy(f32[1024,2,512]{2,1,0:T(2,128)} %reshape_reshape.27) | data formatting | bytes 8388608 | tf_op jit(solution)/shard_map/reshape;reshape | solution.py:89
  192.3 33.3 %all-gather.11.cloned.1.call-done = f32[1,32,32,512]{3,2,0,1:T(8,128)} async-done(((f32[1,2,32,512]{3,2,0,1:T(8,128)}), f32[1,32,32,512]{3,2,0,1:T(8,128)}) %all-gather.11.cloned.1.call-update) | async-done | bytes 2097168 | tf_op jit(solution)/shard_map/all_gather | solution.py:61
  225.6 1.6 fusion.52
  228.7 1.6 fusion.50
  230.3 1.6 fusion.49
  232.0 2.0 copy-done
  234.1 8.6 %bitcast_select_fusion.2 = f32[1024,2,512]{0,2,1:T(8,128)} fusion(f32[1024,2,512]{0,2,1:T(8,128)S(1)} %copy-done, f32[2,512,512]{2,1,0:T(8,128)S(1)} %bitcast.247, pred[1024,2]{0,1:T(4,128)(4,1)S(1)} %get-tuple-element.28, f32[512,512]{1,0:T(8,128)S(1)} %fusion.20, pred[2]{0:T(512)(128)(4,1)S(1)} %select_compare_fusion.1), kind=kOutput, calls=%fused_computation.12 | convolution fusion | flops 6444023808 | bytes 11536386 | tf_op jit(solution)/shard_map/nka,kab->nkb/dot_general | solution.py:20
  242.6 6.6 reshape_reshape.28
  249.2 5.0 fusion.78
  254.2 3.0 copy.155
  259.4 1.6 fusion.47
  261.0 1.6 fusion.46
  262.6 1.6 fusion.45
  264.1 1.6 fusion.44
  265.7 1.6 fusion.43
  267.3 1.6 fusion.42
  268.8 1.6 fusion.41
  270.4 1.6 fusion.40
  273.5 4.2 copy.154
  277.7 4.1 collective-permute-done
  283.1 1.9 maximum_select_fusion
  284.9 12.1 %all-gather.13.cloned.1.call-done = f32[1,2,512,512]{3,2,1,0:T(8,128)} async-done(((f32[1,2,32,512]{3,2,1,0:T(8,128)}), f32[1,2,512,512]{3,2,1,0:T(8,128)}) %all-gather.13.cloned.1.call-update) | async-done | bytes 2097168 | tf_op jit(solution)/shard_map/all_gather | solution.py:60
  297.1 10.6 %fusion.1 = f32[2,512,1024]{2,1,0:T(8,128)S(1)} fusion(f32[2,256,1024]{2,1,0:T(8,128)S(1)} %maximum_select_fusion, f32[2,256,1024]{2,1,0:T(8,128)} %copy.154, pred[2,1024]{1,0:T(4,128)(4,1)S(1)} %get-tuple-element.29, f32[1,2,512,512]{3,2,1,0:T(8,128)} %all-gather.13.cloned.1.call-done, f32[512,512]{1,0:T(8,128)S(1)} %fusion.20, pred[2]{0:T(512)(128)(4,1)S(1)} %fusion.70), kind=kOutput, calls=%fused_computation.14 | convolution fusion | flops 6446120960 | bytes 11536386 | tf_op jit(solution)/shard_map/kab,kan->kbn/dot_general | solution.py:16
  307.7 2.3 fusion.77
  310.0 1.6 fusion.38
  313.1 17.9 %all-to-all-start.1 = ((f32[16,1,1,2,32,512]{5,4,3,2,1,0:T(8,128)}), f32[16,1,1,2,32,512]{5,4,3,2,1,0:T(8,128)}, u32[]{:S(2)}, u32[]{:S(2)}) async-start(f32[16,1,1,2,32,512]{5,4,3,2,1,0:T(8,128)} %fusion.37), calls=%async_computation.1 | async-start | bytes 4194304 | tf_op jit(solution)/shard_map/all_to_all | solution.py:63
  331.1 74.7 %all-gather.7.cloned.1.call-done = f32[1,32,32,512]{3,2,0,1:T(8,128)} async-done(((f32[1,2,32,512]{3,2,0,1:T(8,128)}), f32[1,32,32,512]{3,2,0,1:T(8,128)}) %all-gather.7.cloned.1.call-update) | async-done | bytes 2097168 | tf_op jit(solution)/shard_map/all_gather | solution.py:61
  405.8 1.6 fusion.68
  408.9 1.6 fusion.66
  410.4 1.6 fusion.65
  413.5 1.6 fusion.63
  415.1 1.6 fusion.62
  416.7 1.6 fusion.61
  420.0 2.5 pad_maximum_fusion.1
  422.5 6.6 reshape_reshape.29
  429.1 5.0 fusion.76
  442.1 9.2 %all-to-all-start = ((f32[16,1,1,2,32,512]{5,4,3,2,1,0:T(8,128)}), f32[16,1,1,2,32,512]{5,4,3,2,1,0:T(8,128)}, u32[]{:S(2)}, u32[]{:S(2)}) async-start(f32[16,1,1,2,32,512]{5,4,3,2,1,0:T(8,128)} %fusion.53), calls=%async_computation | async-start | bytes 4194304 | tf_op jit(solution)/shard_map/all_to_all | solution.py:63
  452.5 2.0 copy.126
  454.9 59.6 %collective-permute-done.2 = f32[1024,2,256]{2,0,1:T(8,128)S(1)} collective-permute-done((f32[1024,2,256]{2,0,1:T(8,128)}, f32[1024,2,256]{2,0,1:T(8,128)S(1)}, u32[]{:S(2)}, u32[]{:S(2)}) %collective-permute-start.2) | collective-permute-done | bytes 2097184 | tf_op jit(solution)/shard_map/ppermute | solution.py:12
  514.9 7.7 %bitcast_select_fusion.1 = f32[1024,2,512]{2,0,1:T(8,128)S(1)} fusion(f32[1024,2,256]{2,0,1:T(8,128)S(1)} %maximum_select_fusion.2, f32[1024,2,256]{2,0,1:T(8,128)S(1)} %copy.156, pred[1024,2]{0,1:T(4,128)(4,1)S(1)} %get-tuple-element.27, f32[2,512,512]{2,1,0:T(8,128)S(1)} %bitcast.248, f32[512,512]{1,0:T(8,128)S(1)} %fusion.20, pred[2]{0:T(512)(128)(4,1)S(1)} %fusion.69), kind=kOutput, calls=%fused_computation.11 | convolution fusion | flops 6446120960 | bytes 11536386 | tf_op jit(solution)/shard_map/nka,kab->nkb/dot_general | solution.py:20
  522.7 2.4 fusion.75
  525.1 5.9 collective-permute-start.3
  532.3 18.4 %all-to-all-done = f32[16,1,1,2,32,512]{5,4,3,2,1,0:T(8,128)} async-done(((f32[16,1,1,2,32,512]{5,4,3,2,1,0:T(8,128)}), f32[16,1,1,2,32,512]{5,4,3,2,1,0:T(8,128)}, u32[]{:S(2)}, u32[]{:S(2)}) %all-to-all-start) | async-done | bytes 2097184 | tf_op jit(solution)/shard_map/all_to_all | solution.py:63
  550.7 3.2 copy.124
  553.9 52.2 %collective-permute-done.3 = f32[1024,2,256]{2,0,1:T(8,128)S(1)} collective-permute-done((f32[1024,2,256]{2,0,1:T(8,128)}, f32[1024,2,256]{2,0,1:T(8,128)S(1)}, u32[]{:S(2)}, u32[]{:S(2)}) %collective-permute-start.3) | collective-permute-done | bytes 2097184 | tf_op jit(solution)/shard_map/ppermute | solution.py:12
  608.6 5.3 copy.140
  613.8 6.6 reshape_reshape.30
  620.4 11.6 %convolution_select_fusion = f32[2,512,1024]{2,1,0:T(8,128)} fusion(f32[2,512,1024]{2,1,0:T(8,128)} %reshape_reshape.30, f32[1,2,512,512]{3,2,0,1:T(8,128)} %all-gather.9.cloned.1.call-done, pred[2,1024]{1,0:T(4,128)(4,1)S(1)} %get-tuple-element.30, f32[512,512]{1,0:T(8,128)S(1)} %fusion.20, pred[2]{0:T(512)(128)(4,1)S(1)} %select_compare_fusion.2), kind=kOutput, calls=%fused_computation.16 | convolution fusion | flops 6444023808 | bytes 11536386 | tf_op jit(solution)/shard_map/kab,kan->kbn/dot_general | solution.py:16
  632.0 6.6 reshape_reshape.31
  638.6 7.3 %copy.144 = f32[1024,2,512]{0,2,1:T(8,128)} copy(f32[1024,2,512]{2,1,0:T(2,128)} %reshape_reshape.31) | data formatting | bytes 8388608 | tf_op jit(solution)/shard_map/reshape;reshape | solution.py:89
  646.0 11.8 %bitcast_select_fusion = f32[1024,2,512]{0,2,1:T(8,128)} fusion(f32[1024,2,512]{0,2,1:T(8,128)} %copy.144, f32[2,512,512]{2,1,0:T(8,128)S(1)} %bitcast.246, pred[1024,2]{0,1:T(4,128)(4,1)S(1)} %get-tuple-element.28, f32[512,512]{1,0:T(8,128)S(1)} %fusion.20, pred[2]{0:T(512)(128)(4,1)S(1)} %select_compare_fusion.3), kind=kOutput, calls=%fused_computation.10 | convolution fusion | flops 6444023808 | bytes 11536386 | tf_op jit(solution)/shard_map/nka,kab->nkb/dot_general | solution.py:20
  657.8 5.3 copy.145
  (97 shorter events, 40.2 us)
Async XLA Ops:
  6.5 57.0 %all-gather.15.cloned.1.call-start = ((), (), s32[]{:S(2)}) async-start(), calls=%async_computation.7 | async-start | bytes 2228224 | tf_op jit(solution)/shard_map/all_gather | solution.py:61
  8.4 158.2 %all-gather.17.cloned.1.call-start = ((), (), s32[]{:S(2)}) async-start(), calls=%async_computation.8 | async-start | bytes 2228224 | tf_op jit(solution)/shard_map/all_gather | solution.py:60
  9.2 216.4 %all-gather.11.cloned.1.call-start = ((), (), s32[]{:S(2)}) async-start(), calls=%async_computation.5 | async-start | bytes 2228224 | tf_op jit(solution)/shard_map/all_gather | solution.py:61
  9.9 287.1 %all-gather.13.cloned.1.call-start = ((), (), s32[]{:S(2)}) async-start(), calls=%async_computation.6 | async-start | bytes 2228224 | tf_op jit(solution)/shard_map/all_gather | solution.py:60
  10.5 395.2 %all-gather.7.cloned.1.call-start = ((), (), s32[]{:S(2)}) async-start(), calls=%async_computation.3 | async-start | bytes 2228224 | tf_op jit(solution)/shard_map/all_gather | solution.py:61
  63.5 12.6 %copy-start.7 = (f32[1,32,32,512]{3,2,0,1:T(8,128)S(1)}, f32[1,32,32,512]{3,2,0,1:T(8,128)}, u32[]{:S(2)}) copy-start(f32[1,32,32,512]{3,2,0,1:T(8,128)} %all-gather.15.cloned.1.call-done) | copy-start | bytes 6291460
  81.4 8.3 %copy-start.8 = (s32[3,32]{1,0:T(4,128)S(1)}, s32[3,32]{1,0:T(4,128)}, u32[]{:S(2)}) copy-start(s32[3,32]{1,0:T(4,128)} %param.7) | copy-start | bytes 1156
  81.4 150.4 %all-to-all-start.2 = ((f32[16,1,1,2,32,512]{5,4,3,2,1,0:T(8,128)}), f32[16,1,1,2,32,512]{5,4,3,2,1,0:T(8,128)S(1)}, u32[]{:S(2)}, u32[]{:S(2)}) async-start(f32[16,1,1,2,32,512]{5,4,3,2,1,0:T(8,128)} %fusion.21), calls=%async_computation.2 | async-start | bytes 4194304 | tf_op jit(solution)/shard_map/all_to_all | solution.py:63
  231.9 2.2 copy-start
  257.3 24.5 %collective-permute-start = (f32[2,256,1024]{2,1,0:T(8,128)}, f32[2,256,1024]{2,1,0:T(8,128)S(1)}, u32[]{:S(2)}, u32[]{:S(2)}) collective-permute-start(f32[2,256,1024]{2,1,0:T(8,128)} %copy.155), channel_id=1, source_target_pairs={{0,240},{16,0},{32,16},{48,32},{64,48},{80,64},{96,80},{112,96},{1... | collective-permute-start | bytes 6291464 | tf_op jit(solution)/shard_map/ppermute | solution.py:12
  281.8 1.3 copy-start.1
  310.0 108.2 %collective-permute-start.1 = (f32[2,256,1024]{2,1,0:T(8,128)}, f32[2,256,1024]{2,1,0:T(8,128)S(1)}, u32[]{:S(2)}, u32[]{:S(2)}) collective-permute-start(f32[2,256,1024]{2,1,0:T(8,128)} %get-tuple-element.10), channel_id=1, source_target_pairs={{0,16},{16,32},{32,48},{48,64},{64,80},{80,96},{96,112},{112,128},... | collective-permute-start | bytes 6291464 | tf_op jit(solution)/shard_map/ppermute | solution.py:12
  313.1 129.0 %all-to-all-start.1 = ((f32[16,1,1,2,32,512]{5,4,3,2,1,0:T(8,128)}), f32[16,1,1,2,32,512]{5,4,3,2,1,0:T(8,128)}, u32[]{:S(2)}, u32[]{:S(2)}) async-start(f32[16,1,1,2,32,512]{5,4,3,2,1,0:T(8,128)} %fusion.37), calls=%async_computation.1 | async-start | bytes 4194304 | tf_op jit(solution)/shard_map/all_to_all | solution.py:63
  418.4 1.6 copy-start.4
  434.1 2.8 copy-start.6
  435.6 78.9 %collective-permute-start.2 = (f32[1024,2,256]{2,0,1:T(8,128)}, f32[1024,2,256]{2,0,1:T(8,128)S(1)}, u32[]{:S(2)}, u32[]{:S(2)}) collective-permute-start(f32[1024,2,256]{2,0,1:T(8,128)} %copy.157), channel_id=1, source_target_pairs={{0,15},{1,0},{2,1},{3,2},{4,3},{5,4},{6,5},{7,6},{8,7},{9,8},{10,9... | collective-permute-start | bytes 6291464 | tf_op jit(solution)/shard_map/ppermute | solution.py:12
  442.1 108.6 %all-to-all-start = ((f32[16,1,1,2,32,512]{5,4,3,2,1,0:T(8,128)}), f32[16,1,1,2,32,512]{5,4,3,2,1,0:T(8,128)}, u32[]{:S(2)}, u32[]{:S(2)}) async-start(f32[16,1,1,2,32,512]{5,4,3,2,1,0:T(8,128)} %fusion.53), calls=%async_computation | async-start | bytes 4194304 | tf_op jit(solution)/shard_map/all_to_all | solution.py:63
  451.3 169.1 %all-gather.9.cloned.1.call-start = ((), (), s32[]{:S(2)}) async-start(), calls=%async_computation.4 | async-start | bytes 2228224 | tf_op jit(solution)/shard_map/all_gather | solution.py:60
  452.5 2.2 copy-start.2
  525.1 81.1 %collective-permute-start.3 = (f32[1024,2,256]{2,0,1:T(8,128)}, f32[1024,2,256]{2,0,1:T(8,128)S(1)}, u32[]{:S(2)}, u32[]{:S(2)}) collective-permute-start(f32[1024,2,256]{2,0,1:T(8,128)} %get-tuple-element.6), channel_id=1, source_target_pairs={{0,1},{1,2},{2,3},{3,4},{4,5},{5,6},{6,7},{7,8},{8,9},{9,10},{10,1... | collective-permute-start | bytes 6291464 | tf_op jit(solution)/shard_map/ppermute | solution.py:12
  606.3 1.6 copy-start.5
  638.6 7.3 %copy-start.3 = (f32[1,1,2,16,32,512]{5,4,3,2,1,0:T(8,128)S(1)}, f32[1,1,2,16,32,512]{5,4,3,2,1,0:T(8,128)}, u32[]{:S(2)}) copy-start(f32[1,1,2,16,32,512]{5,4,3,2,1,0:T(8,128)} %copy.124) | copy-start | bytes 6291460
Sparse Core Ops, SparseCore 0:
  10.1 53.3 all-gather.14
  65.3 101.3 all-gather.16
  169.4 56.1 all-gather.10
  227.3 69.7 all-gather.12
  299.7 106.0 all-gather.6
  453.6 154.5 all-gather.8
